TPU v7x, 256 devices: a whole 4x4x8 slice. The times are simulated.
256 devices in a mesh: wide: 32 (over z, x_lo, core), req: 8 (over y, x_hi).
Axes of the slice: x: 4 (x_hi: 2, x_lo: 2; x = x_hi * 2 + x_lo), y: 4, z: 8, core: 2. Of those that a mesh axis runs over, the one named last changes fastest.
Arguments:
- x_in: bfloat16 [2048, 8192], P('req', 'wide'), may hold values from -6 to 6
- w_xz: bfloat16 [8192, 2, 16384], P('req', None, 'wide'), may hold values from -0.0625 to 0.0625
- w_dt: bfloat16 [8192, 256], P('req', 'wide'), may hold values from -0.0625 to 0.0625
- w_bc: bfloat16 [8192, 4096], P('req', 'wide'), may hold values from -0.0625 to 0.0625
- dt_bias: float32 [256], P('wide'), may hold values from -7 to -3
- a_log: float32 [256], P('wide'), may hold values from 0 to 2.77
- d_skip: float32 [256], P('wide'), may hold values from 0.5 to 1.5
- conv_x_w: float32 [4, 16384], P(None, 'wide'), may hold values from -3 to 3
- conv_x_b: float32 [16384], P('wide'), may hold values from -3 to 3
- conv_bc_w: float32 [4, 4096], P(None, 'wide'), may hold values from -3 to 3
- conv_bc_b: float32 [4096], P('wide'), may hold values from -3 to 3
- norm_gain: float32 [16384], P('wide'), may hold values from 0.5 to 1.5
- stretch_start: int32 [8, 2], P('req'), may hold values from 0 to 255, as said below
- prefix_len: int32 [16], P('req'), may hold values from 0 to 32768, as said below
- state_slot: int32 [16], replicated, may hold values from 0 to 63, as said below
- ssm_pool: float32 [64, 256, 64, 256], P('req', 'wide'), may hold values from -6 to 6
- conv_x_pool: bfloat16 [64, 3, 16384], P('req', None, 'wide'), may hold values from -6 to 6
- conv_bc_pool: bfloat16 [64, 3, 4096], P('req', None, 'wide'), may hold values from -6 to 6
Outputs:
- y_out: bfloat16 [2048, 16384], P('req', 'wide')
- new_state: float32 [16, 256, 64, 256], P('req', 'wide')
Inputs may be any that keep to these rules, and one draw needn't show every extreme that they name: `stretch_start`: each row is 0 first and rises strictly; the 2 requests of an index of req cover its 256 tokens in order. `prefix_len`: zero means no cached state; in every draw some request has zero and one has 32768. `state_slot`: distinct slots; slot s is owned by index s // 8 of req; owners hold very uneven numbers of the requested slots.
All inputs are finite; a program needn't handle non-finite values.
Results may differ from a plain program's by a relative error of at most 0.014.
Values may be sent and summed in bfloat16 or wider, within the bound.
A program may use at most 128 MiB of HBM per device.

v0:
```python
import jax
import jax.numpy as jnp
from jax import lax
from jax.sharding import PartitionSpec as P

HEADS = 256
HEAD_DIM = 64
GROUPS = 8
NORM_EPS = 1e-05


def partner_2(block, axis, bit):
    count = lax.axis_size(axis)
    route = []
    for low in range(count):
        high = low | 1 << bit
        if high != low and high < count:
            route += [(low, high), (high, low)]
    return lax.ppermute(block, axis, route)


def segments(starts, count_tok):
    position = jnp.arange(count_tok, dtype=jnp.int32)
    seg_ids = jnp.sum((position[:, None] >= starts[None, :]).astype(jnp.int32), 1) - 1
    member = seg_ids[:, None] == jnp.arange(starts.shape[0], dtype=jnp.int32)[None, :]
    offset = position - jnp.sum(jnp.where(member, starts[None, :], 0), 1)
    same_req = seg_ids[:, None] == seg_ids[None, :]
    causal = position[:, None] >= position[None, :]
    return (member.astype(jnp.float32), offset, (same_req & causal).astype(jnp.float32))


def causal_conv(inputs, cache, kernel, bias, member, offset):
    kernel_len = kernel.shape[0]
    count_tok, channels = inputs.shape
    count_req = cache.shape[0]
    history = jnp.dot(
        member,
        cache.reshape(count_req, (kernel_len - 1) * channels),
        precision=lax.Precision.HIGHEST,
    )
    history = history.reshape(count_tok, kernel_len - 1, channels)
    values = inputs.astype(jnp.float32)
    total = bias[None, :] + kernel[kernel_len - 1][None, :] * values
    for lag_step in range(1, kernel_len):
        shifted = jnp.concatenate(
            [jnp.zeros((lag_step, channels), jnp.float32), values[: count_tok - lag_step]], 0
        )
        earlier = jnp.zeros((count_tok, channels), jnp.float32)
        for slot_place in range(kernel_len - 1):
            hit_place = offset - lag_step + kernel_len - 1 == slot_place
            earlier = earlier + jnp.where(hit_place[:, None], history[:, slot_place], 0.0)
        chosen = jnp.where((offset >= lag_step)[:, None], shifted, earlier)
        total = total + kernel[kernel_len - 1 - lag_step][None, :] * chosen
    return jax.nn.silu(total).astype(jnp.bfloat16)


def mixer(inputs, dt_raw, b_maps, c_maps, start_state, member, mask, dt_bias, a_log, d_skip):
    high = lax.Precision.HIGHEST
    step_size = jax.nn.softplus(dt_raw.astype(jnp.float32) + dt_bias[None, :])
    decay_rate = step_size * (-jnp.exp(a_log))[None, :]
    cumulative = jnp.dot(mask, decay_rate, precision=high)
    scores = jnp.dot(c_maps, b_maps.T, preferred_element_type=jnp.float32)
    spread_gap = jnp.minimum(cumulative.T[:, :, None] - cumulative.T[:, None, :], 0.0)
    decay = jnp.exp(spread_gap) * mask[None] * step_size.T[:, None, :]
    weights = (decay * scores[None]).astype(jnp.bfloat16)
    intra = jnp.einsum("hts,shp->thp", weights, inputs, preferred_element_type=jnp.float32)
    values = inputs.astype(jnp.float32)
    from_state = jnp.einsum(
        "tn,jhpn->jthp", c_maps.astype(jnp.float32), start_state, precision=high
    )
    from_state = jnp.einsum("tj,jthp->thp", member, from_state, precision=high)
    from_state = from_state * jnp.exp(cumulative)[:, :, None]
    result = intra + from_state + d_skip[None, :, None] * values
    ends = jnp.dot(member.T, decay_rate, precision=high)
    to_end = jnp.exp(jnp.dot(member, ends, precision=high) - cumulative)
    carried = (to_end * step_size)[:, :, None] * values
    split_req = (member.T[:, :, None, None] * carried[None]).astype(jnp.bfloat16)
    fresh = jnp.einsum("jthp,tn->jhpn", split_req, b_maps, preferred_element_type=jnp.float32)
    final_state = jnp.exp(ends)[:, :, None, None] * start_state + fresh
    return (result, final_state)


def on_device(
    x_in,
    w_xz,
    w_dt,
    w_bc,
    dt_bias,
    a_log,
    d_skip,
    conv_x_w,
    conv_x_b,
    conv_bc_w,
    conv_bc_b,
    norm_gain,
    stretch_start,
    prefix_len,
    state_slot,
    ssm_pool,
    conv_x_pool,
    conv_bc_pool,
):
    features = lax.all_gather(x_in, "wide", axis=1, tiled=True)
    count_tok = features.shape[0]
    local_width = w_xz.shape[2]
    local_heads = w_dt.shape[1]
    acc_xz = jnp.einsum(
        "td,dkc->tkc",
        features,
        lax.all_gather(w_xz, "req", axis=0, tiled=True),
        preferred_element_type=jnp.float32,
    )
    acc_dt = jnp.dot(
        features,
        lax.all_gather(w_dt, "req", axis=0, tiled=True),
        preferred_element_type=jnp.float32,
    )
    acc_bc = jnp.dot(
        features,
        lax.all_gather(w_bc, "req", axis=0, tiled=True),
        preferred_element_type=jnp.float32,
    )
    proj_xz = acc_xz.astype(jnp.bfloat16)
    dt_raw = acc_dt.astype(jnp.bfloat16)
    bc_raw = acc_bc.astype(jnp.bfloat16)
    owner = lax.axis_index("req")
    req_count = lax.axis_size("req")
    slot_count = conv_x_pool.shape[0]
    local_slot = jnp.clip(state_slot - owner * slot_count, 0, slot_count - 1)
    is_owner = state_slot // slot_count == owner
    send_ssm = jnp.where(is_owner[:, None, None, None], ssm_pool[local_slot], 0.0)
    send_cx = jnp.where(is_owner[:, None, None], conv_x_pool[local_slot].astype(jnp.float32), 0.0)
    send_cbc = jnp.where(is_owner[:, None, None], conv_bc_pool[local_slot].astype(jnp.float32), 0.0)
    got_ssm, got_cx, got_cbc = (
        lax.all_to_all(send_ssm, "req", split_axis=0, concat_axis=0, tiled=True),
        lax.all_to_all(send_cx, "req", split_axis=0, concat_axis=0, tiled=True),
        lax.all_to_all(send_cbc, "req", split_axis=0, concat_axis=0, tiled=True),
    )
    group_reqs = prefix_len.shape[0]
    has_cache = (prefix_len > 0).astype(jnp.float32)
    start_state = (
        jnp.sum(got_ssm.reshape((req_count, group_reqs) + got_ssm.shape[1:]), 0)
        * has_cache[:, None, None, None]
    )
    cache_x = (
        jnp.sum(got_cx.reshape((req_count, group_reqs) + got_cx.shape[1:]), 0)
        * has_cache[:, None, None]
    )
    cache_bc = (
        jnp.sum(got_cbc.reshape((req_count, group_reqs) + got_cbc.shape[1:]), 0)
        * has_cache[:, None, None]
    )
    member, offset, mask = segments(stretch_start[0], count_tok)
    x_conv = causal_conv(proj_xz[:, 1], cache_x, conv_x_w, conv_x_b, member, offset)
    bc_conv = causal_conv(bc_raw, cache_bc, conv_bc_w, conv_bc_b, member, offset)
    wide_index = lax.axis_index("wide")
    group_span = lax.axis_size("wide") // GROUPS
    bit_total = group_span.bit_length() - 1
    joined = bc_conv
    for bit_index in range(bit_total):
        partner = partner_2(joined, "wide", bit_index)
        upper_half = wide_index // (1 << bit_index) % 2 == 1
        joined = jnp.where(
            upper_half, jnp.concatenate([partner, joined], 1), jnp.concatenate([joined, partner], 1)
        )
    state_width = joined.shape[1] // 2
    b_maps = joined[:, :state_width]
    c_maps = joined[:, state_width:]
    head_width = local_width // local_heads
    result, final_state = mixer(
        x_conv.reshape(count_tok, local_heads, head_width),
        dt_raw,
        b_maps,
        c_maps,
        start_state,
        member,
        mask,
        dt_bias,
        a_log,
        d_skip,
    )
    gated = result.reshape(count_tok, local_width) * jax.nn.silu(proj_xz[:, 0].astype(jnp.float32))
    square_sum = jnp.sum(gated * gated, 1)
    for bit_index in range(bit_total):
        square_sum = square_sum + partner_2(square_sum, "wide", bit_index)
    mean_sq = square_sum / (HEADS * HEAD_DIM // GROUPS)
    normed = gated * lax.rsqrt(mean_sq + NORM_EPS)[:, None] * norm_gain[None, :]
    return (normed.astype(jnp.bfloat16), final_state)


def solution(mesh):
    in_specs = (
        P("req", "wide"),
        P("req", None, "wide"),
        P("req", "wide"),
        P("req", "wide"),
        P("wide"),
        P("wide"),
        P("wide"),
        P(None, "wide"),
        P("wide"),
        P(None, "wide"),
        P("wide"),
        P("wide"),
        P("req", None),
        P("req"),
        P(),
        P("req", "wide", None, None),
        P("req", None, "wide"),
        P("req", None, "wide"),
    )
    out_specs = (P("req", "wide"), P("req", "wide", None, None))
    return jax.shard_map(
        on_device, mesh=mesh, in_specs=in_specs, out_specs=out_specs, check_vma=False
    )
```

profile of v0, /device:TPU:1, one launch (start us, length us, event | category | flops | bytes accessed | tf_op | source)
XLA Modules:
  0.0 421.8 jit_solution(5018810072848733110)
XLA Ops:
  8.7 3.2 copy.42
  13.4 7.5 %all-to-all-start.1 = ((f32[16,3,128]{2,1,0:T(4,128)}), f32[16,3,128]{2,1,0:T(4,128)S(1)}, u32[]{:S(2)}, u32[]{:S(2)}) async-start(f32[16,3,128]{2,1,0:T(4,128)} %copy.47), calls=%async_computation.1 | async-start | bytes 65536 | tf_op jit(solution)/shard_map/all_to_all | solution.py:137
  21.6 0.7 copy.43
  22.4 6.5 %gather_fusion.2 = f32[16,8,64,256]{3,2,1,0:T(8,128)} fusion(f32[8,8,64,256]{3,2,1,0:T(8,128)} %param.33, s32[1024]{0:T(1024)S(1)} %pad_clamp_fusion), kind=kCustom, calls=%fused_computation.2 | custom fusion | bytes 16777280 | tf_op jit(solution)/shard_map/gather | solution.py:131
  28.9 6.6 %all-to-all-start = ((f32[16,3,512]{2,1,0:T(4,128)}), f32[16,3,512]{2,1,0:T(4,128)S(1)}, u32[]{:S(2)}, u32[]{:S(2)}) async-start(f32[16,3,512]{2,1,0:T(4,128)} %copy.43), calls=%async_computation | async-start | bytes 262144 | tf_op jit(solution)/shard_map/all_to_all | solution.py:136
  35.5 8.4 %broadcast_select_fusion = f32[16,8,64,256]{3,2,1,0:T(8,128)} fusion(f32[16,8,64,256]{3,2,1,0:T(8,128)} %gather_fusion.2, pred[16]{0:T(512)(128)(4,1)S(1)} %fusion.71), kind=kLoop, calls=%fused_computation.5 | loop fusion | flops 2097152 | bytes 16777232 | tf_op jit(solution)/shard_map/jit(_where)/select_n | solution.py:131
  44.0 6.8 %all-to-all-start.2 = ((f32[16,8,64,256]{3,2,1,0:T(8,128)}), f32[16,8,64,256]{3,2,1,0:T(8,128)}, u32[]{:S(2)}, u32[]{:S(2)}) async-start(f32[16,8,64,256]{3,2,1,0:T(8,128)} %broadcast_select_fusion), calls=%async_computation.2 | async-start | bytes 16777216 | tf_op jit(solution)/shard_map/all_to_all | solution.py:135
  50.8 137.9 %all_gather.14 = bf16[8192,8]{0,1:T(8,128)(2,1)S(1)} all-gather(bf16[1024,8]{0,1:T(8,128)(2,1)S(1)} %copy-done.4), channel_id=1, replica_groups=mesh['wide'=32,'req'=8] {'req'}, dimensions={0}, use_global_device_ids=true | all-gather | bytes 147456 | tf_op jit(solution)/shard_map/all_gather | solution.py:115
  189.0 0.8 fusion.36
  190.4 0.8 fusion.59
  191.2 4.3 %reduce_sum.64 = f32[2,8,64,256]{3,2,1,0:T(8,128)S(1)} reduce(f32[8,2,8,64,256]{4,3,2,1,0:T(8,128)} %bitcast.33, f32[]{:T(128)} %constant.94.clone.1), dimensions={0}, to_apply=%region_4.5 | reduce | flops 1835008 | bytes 9437188 | tf_op jit(solution)/shard_map/reduce_sum | solution.py:142
  195.5 2.7 all-gather.4.cloned.1.call-done
  198.2 4.5 %fusion.7 = f32[256,128]{0,1:T(8,128)S(1)} fusion(bf16[256,8192]{1,0:T(8,128)(2,1)} %all-gather.4.cloned.1.call-done, bf16[8192,128]{1,0:T(8,128)(2,1)} %all-gather.8.cloned.1.call-done), kind=kOutput, calls=%fused_computation.13 | convolution fusion | flops 536936448 | bytes 6422528 | tf_op jit(solution)/shard_map/dot_general | solution.py:118
  203.1 5.2 %collective-permute-start = (bf16[256,128]{0,1:T(8,128)(2,1)S(1)}, bf16[256,128]{0,1:T(8,128)(2,1)S(1)}, u32[]{:S(2)}, u32[]{:S(2)}) collective-permute-start(bf16[256,128]{0,1:T(8,128)(2,1)S(1)} %multiply_convert_fusion.5), channel_id=1, source_target_pairs={{0,8},{8,0},{16,24},{24,16},{32,40},{40,32},{48,56},{56,48},{64,72... | collective-permute-start | bytes 196616 | tf_op jit(solution)/shard_map/ppermute | solution.py:19
  208.2 1.2 compare_select_fusion
  210.5 4.8 %collective-permute-done.1 = bf16[256,256]{0,1:T(8,128)(2,1)S(1)} collective-permute-done((bf16[256,256]{0,1:T(8,128)(2,1)S(1)}, bf16[256,256]{0,1:T(8,128)(2,1)S(1)}, u32[]{:S(2)}, u32[]{:S(2)}) %collective-permute-start.1) | collective-permute-done | bytes 131104 | tf_op jit(solution)/shard_map/ppermute | solution.py:19
  216.1 0.9 fusion.12
  217.1 0.9 fusion.44
  218.0 168.4 %all-gather.6.cloned.1.call-done = bf16[8192,2,512]{2,0,1:T(8,128)(2,1)} async-done(((bf16[1024,2,512]{2,0,1:T(8,128)(2,1)}), bf16[8192,2,512]{2,0,1:T(8,128)(2,1)}) %all-gather.6.cloned.1.call-update) | async-done | bytes 16777232 | tf_op jit(solution)/shard_map/all_gather | solution.py:110
  386.4 11.5 %fusion.2 = bf16[256,2,512]{2,0,1:T(8,128)(2,1)S(1)} fusion(bf16[8192,2,512]{2,0,1:T(8,128)(2,1)} %all-gather.6.cloned.1.call-done, bf16[256,8192]{1,0:T(8,128)(2,1)} %all-gather.4.cloned.1.call-done), kind=kOutput, calls=%fused_computation.8 | convolution fusion | flops 4295229440 | bytes 21495808 | tf_op jit(solution)/shard_map/td,dkc->tkc/dot_general | solution.py:107
  397.9 0.9 slice_convert_fusion
  398.8 0.8 slice_bitcast_fusion
  399.6 0.8 slice_bitcast_fusion.1
  400.4 0.8 slice_bitcast_fusion.5
  401.3 2.0 copy.52
  403.3 3.0 multiply_convert_fusion.4
  406.3 1.1 copy.46
  407.4 2.2 multiply_reduce_fusion
  409.7 1.5 collective-permute-start.2
  411.2 0.8 collective-permute-done.2
  412.3 1.3 convolution_add_fusion
  414.4 0.9 fusion.34
  (80 shorter events, 7.8 us)
Async XLA Ops:
  7.2 13.7 %copy-start = (bf16[8,3,512]{2,0,1:T(8,128)(2,1)S(1)}, bf16[8,3,512]{2,0,1:T(8,128)(2,1)}, u32[]{:S(2)}) copy-start(bf16[8,3,512]{2,0,1:T(8,128)(2,1)} %param.34) | copy-start | bytes 73732
  7.2 4.8 %copy-start.12 = (s32[16]{0:T(128)S(1)}, s32[16]{0:T(128)}, u32[]{:S(2)}) copy-start(s32[16]{0:T(128)} %param.32) | copy-start | bytes 196
  7.2 4.8 %copy-start.3 = (bf16[8,3,128]{2,0,1:T(8,128)(2,1)S(1)}, bf16[8,3,128]{2,0,1:T(8,128)(2,1)}, u32[]{:S(2)}) copy-start(bf16[8,3,128]{2,0,1:T(8,128)(2,1)} %param.35) | copy-start | bytes 18436
  7.2 188.3 %all-gather.8.cloned.1.call-start = ((), (), s32[]{:S(2)}) async-start(), calls=%async_computation.5 | async-start | bytes 2359296 | tf_op jit(solution)/shard_map/all_gather | solution.py:120
  7.9 190.3 %all-gather.4.cloned.1.call-start = ((), (), s32[]{:S(2)}) async-start(), calls=%async_computation.3 | async-start | bytes 4325376 | tf_op jit(solution)/shard_map/all_gather | solution.py:103
  8.7 377.7 %all-gather.6.cloned.1.call-start = ((), (), s32[]{:S(2)}) async-start(), calls=%async_computation.4 | async-start | bytes 18874368 | tf_op jit(solution)/shard_map/all_gather | solution.py:110
  13.4 15.5 %all-to-all-start.1 = ((f32[16,3,128]{2,1,0:T(4,128)}), f32[16,3,128]{2,1,0:T(4,128)S(1)}, u32[]{:S(2)}, u32[]{:S(2)}) async-start(f32[16,3,128]{2,1,0:T(4,128)} %copy.47), calls=%async_computation.1 | async-start | bytes 65536 | tf_op jit(solution)/shard_map/all_to_all | solution.py:137
  28.9 15.1 %all-to-all-start = ((f32[16,3,512]{2,1,0:T(4,128)}), f32[16,3,512]{2,1,0:T(4,128)S(1)}, u32[]{:S(2)}, u32[]{:S(2)}) async-start(f32[16,3,512]{2,1,0:T(4,128)} %copy.43), calls=%async_computation | async-start | bytes 262144 | tf_op jit(solution)/shard_map/all_to_all | solution.py:136
  44.0 6.8 %copy-start.4 = (bf16[1024,8]{0,1:T(8,128)(2,1)S(1)}, bf16[1024,8]{0,1:T(8,128)(2,1)}, u32[]{:S(2)}) copy-start(bf16[1024,8]{0,1:T(8,128)(2,1)} %param.20) | copy-start | bytes 49156
  44.0 144.7 %copy-start.11 = (s32[1,2]{1,0:T(1,128)S(1)}, s32[1,2]{1,0:T(1,128)}, u32[]{:S(2)}) copy-start(s32[1,2]{1,0:T(1,128)} %param.30) | copy-start | bytes 28
  44.0 144.9 %copy-start.13 = (s32[2]{0:T(128)S(1)}, s32[2]{0:T(128)}, u32[]{:S(2)}) copy-start(s32[2]{0:T(128)} %param.31) | copy-start | bytes 28
  44.0 144.9 %copy-start.14 = (f32[8]{0:T(128)S(1)}, f32[8]{0:T(128)}, u32[]{:S(2)}) copy-start(f32[8]{0:T(128)} %param.23) | copy-start | bytes 100
  44.0 144.9 %copy-start.9 = (f32[4,128]{1,0:T(4,128)S(1)}, f32[4,128]{1,0:T(4,128)}, u32[]{:S(2)}) copy-start(f32[4,128]{1,0:T(4,128)} %param.27) | copy-start | bytes 6148
  44.0 144.9 %copy-start.5 = (f32[4,512]{1,0:T(4,128)S(1)}, f32[4,512]{1,0:T(4,128)}, u32[]{:S(2)}) copy-start(f32[4,512]{1,0:T(4,128)} %param.25) | copy-start | bytes 24580
  44.0 147.2 %all-to-all-start.2 = ((f32[16,8,64,256]{3,2,1,0:T(8,128)}), f32[16,8,64,256]{3,2,1,0:T(8,128)}, u32[]{:S(2)}, u32[]{:S(2)}) async-start(f32[16,8,64,256]{3,2,1,0:T(8,128)} %broadcast_select_fusion), calls=%async_computation.2 | async-start | bytes 16777216 | tf_op jit(solution)/shard_map/all_to_all | solution.py:135
  195.5 7.2 %copy-start.10 = (f32[128]{0:T(128)S(1)}, f32[128]{0:T(128)}, u32[]{:S(2)}) copy-start(f32[128]{0:T(128)} %param.28) | copy-start | bytes 1540
  195.5 12.7 %copy-start.8 = (f32[8]{0:T(128)S(1)}, f32[8]{0:T(128)}, u32[]{:S(2)}) copy-start(f32[8]{0:T(128)} %param.22) | copy-start | bytes 100
  198.2 10.0 %copy-start.2 = (bf16[256,8192]{1,0:T(8,128)(2,1)S(1)}, bf16[256,8192]{1,0:T(8,128)(2,1)}, u32[]{:S(2)}) copy-start(bf16[256,8192]{1,0:T(8,128)(2,1)} %all-gather.4.cloned.1.call-done) | copy-start | bytes 12582916
  203.1 6.9 %collective-permute-start = (bf16[256,128]{0,1:T(8,128)(2,1)S(1)}, bf16[256,128]{0,1:T(8,128)(2,1)S(1)}, u32[]{:S(2)}, u32[]{:S(2)}) collective-permute-start(bf16[256,128]{0,1:T(8,128)(2,1)S(1)} %multiply_convert_fusion.5), channel_id=1, source_target_pairs={{0,8},{8,0},{16,24},{24,16},{32,40},{40,32},{48,56},{56,48},{64,72... | collective-permute-start | bytes 196616 | tf_op jit(solution)/shard_map/ppermute | solution.py:19
  210.0 5.3 %collective-permute-start.1 = (bf16[256,256]{0,1:T(8,128)(2,1)S(1)}, bf16[256,256]{0,1:T(8,128)(2,1)S(1)}, u32[]{:S(2)}, u32[]{:S(2)}) collective-permute-start(bf16[256,256]{0,1:T(8,128)(2,1)S(1)} %maximum_select_fusion.1), channel_id=1, source_target_pairs={{0,16},{16,0},{8,24},{24,8},{32,48},{48,32},{40,56},{56,40},{64,80... | collective-permute-start | bytes 393224 | tf_op jit(solution)/shard_map/ppermute | solution.py:19
  397.9 5.4 %copy-start.6 = (f32[512]{0:T(512)S(1)}, f32[512]{0:T(512)}, u32[]{:S(2)}) copy-start(f32[512]{0:T(512)} %param.26) | copy-start | bytes 6148
  398.8 8.6 %copy-start.15 = (f32[8]{0:T(128)S(1)}, f32[8]{0:T(128)}, u32[]{:S(2)}) copy-start(f32[8]{0:T(128)} %param.24) | copy-start | bytes 100
  407.4 7.0 %copy-start.7 = (f32[512]{0:T(512)S(1)}, f32[512]{0:T(512)}, u32[]{:S(2)}) copy-start(f32[512]{0:T(512)} %param.29) | copy-start | bytes 6148
  407.4 7.9 %copy-start.1 = (bf16[8,3,512]{2,0,1:T(8,128)(2,1)S(1)}, bf16[8,3,512]{2,0,1:T(8,128)(2,1)}, u32[]{:S(2)}) copy-start(bf16[8,3,512]{2,0,1:T(8,128)(2,1)} %param.34) | copy-start | bytes 73732
  409.7 2.3 collective-permute-start.2
  412.0 2.4 collective-permute-start.3
Sparse Core Ops, SparseCore 0:
  10.7 75.4 all-gather.7
  87.9 110.2 all-gather.3
  200.8 185.4 all-gather.5
where the time goes:
time: 422 us
  waiting for transfers between devices  179 us (42%)
  blocking collectives  138 us (33%)
  starting transfers between devices  28.2 us (7%)
  matrix products  24.4 us (6%)
  other arithmetic  20.2 us (5%)
  local copies, waits for them, and re-layouts  18.4 us (4%)
  between operations  14.1 us (3%)
    all_gather x1, waiting for transfers between devices, on_device(): lax.all_gather(w_xz, 'req', axis=0, tiled=True)  168 us
    all_gather x1, blocking collectives, on_device(): lax.all_gather(w_dt, 'req', axis=0, tiled=True)  138 us
    dot_general x1, matrix products, on_device(): jnp.einsum('td,dkc->tkc', features, lax.all_gather(w_xz, 'req', axis=0, t...  11.5 us
    select_n x1, other arithmetic, on_device(): jnp.where(is_owner[:, None, None, None], ssm_pool[local_slot], 0.0)  8.44 us
  transfers between devices with their start and end apart: 10, of which 5 were waited for; matrix products, arithmetic and copies ran while one was open for 9% of the time, Pallas kernels for 0%

commit v1 on v0

--- a/solution.py
+++ b/solution.py
@@ -7,6 +7,11 @@
 HEAD_DIM = 64
 GROUPS = 8
 NORM_EPS = 1e-05
+
+
+def swapped_in(x, name, d):
+    stack = jnp.stack([x] * lax.axis_size(name))
+    return jnp.concatenate(lax.all_to_all(stack, name, 0, 0), axis=d)
 
 
 def partner_2(block, axis, bit):
@@ -105,10 +110,7 @@
     local_width = w_xz.shape[2]
     local_heads = w_dt.shape[1]
     acc_xz = jnp.einsum(
-        "td,dkc->tkc",
-        features,
-        lax.all_gather(w_xz, "req", axis=0, tiled=True),
-        preferred_element_type=jnp.float32,
+        "td,dkc->tkc", features, swapped_in(w_xz, "req", 0), preferred_element_type=jnp.float32
     )
     acc_dt = jnp.dot(
         features,

time: 422 us -> 483 us (1.14)
  blocking collectives: 138 us -> 217 us
  waiting for transfers between devices: 179 us -> 150 us
  local copies, waits for them, and re-layouts: 18.4 us -> 31.9 us
  matrix products: 24.4 us -> 17.4 us
    all_gather x1 -> x0, waiting for transfers between devices: 168 us -> none  [on_device(): lax.all_gather(w_xz, 'req', axis=0, tiled=True)]
    all_to_all x1, waiting for transfers between devices: 0.01 us -> 92 us  [on_device(): lax.all_to_all(send_ssm, 'req', split_axis=0, concat_axis=0, tiled=True)]
    all_gather x1, blocking collectives: 138 us -> 217 us  [on_device(): lax.all_gather(w_dt, 'req', axis=0, tiled=True)]
    all_gather x1, waiting for transfers between devices: 2.68 us -> 51.7 us  [on_device(): features = lax.all_gather(x_in, 'wide', axis=1, tiled=True)]
    all_to_all x0 -> x1, local copies, waits for them, and re-layouts: none -> 8.24 us  [swapped_in(): return jnp.concatenate(lax.all_to_all(stack, name, 0, 0), axis=d)]
    dot_general x1, matrix products: 11.5 us -> 4.52 us  [on_device(): jnp.einsum('td,dkc->tkc', features, swapped_in(w_xz, 'req', 0), preferred...]
    another operation x0 -> x1, local copies, waits for them, and re-layouts: none -> 5.89 us  [swapped_in(): stack = jnp.stack([x] * lax.axis_size(name))]
    all_to_all x0 -> x1, starting transfers between devices: none -> 5.89 us  [swapped_in(): return jnp.concatenate(lax.all_to_all(stack, name, 0, 0), axis=d)]
  transfers between devices with their start and end apart: 10 -> 10, of which waited for: 5 -> 4; matrix products, arithmetic and copies ran while one was open for 9% -> 7% of each run, Pallas kernels for 0% -> 0%
where the time goes in v1:
time: 483 us; the launch traced here: 482 us
  blocking collectives  217 us (45%)
  waiting for transfers between devices  150 us (31%)
  local copies, waits for them, and re-layouts  31.9 us (7%)
  starting transfers between devices  30.4 us (6%)
  other arithmetic  21.5 us (4%)
  matrix products  17.4 us (4%)
  between operations  14.4 us (3%)
    all_gather x1, blocking collectives, on_device(): lax.all_gather(w_dt, 'req', axis=0, tiled=True)  217 us
    all_to_all x1, waiting for transfers between devices, on_device(): lax.all_to_all(send_ssm, 'req', split_axis=0, concat_axis=0, tiled=True)  92 us
    all_gather x1, waiting for transfers between devices, on_device(): features = lax.all_gather(x_in, 'wide', axis=1, tiled=True)  51.7 us
  transfers between devices with their start and end apart: 10, of which 4 were waited for; matrix products, arithmetic and copies ran while one was open for 7% of the time, Pallas kernels for 0%

profile of v1, /device:TPU:1, one launch (start us, length us, event | category | flops | bytes accessed | tf_op | source)
XLA Modules:
  0.0 482.3 jit_solution(16611814541089707031)
XLA Ops:
  8.5 1.3 gather_fusion.1
  10.5 7.5 %all-to-all-start.2 = ((f32[16,3,128]{2,1,0:T(4,128)}), f32[16,3,128]{2,1,0:T(4,128)S(1)}, u32[]{:S(2)}, u32[]{:S(2)}) async-start(f32[16,3,128]{2,1,0:T(4,128)} %copy.48), calls=%async_computation.2 | async-start | bytes 65536 | tf_op jit(solution)/shard_map/all_to_all | solution.py:139
  19.5 6.5 %gather_fusion.2 = f32[16,8,64,256]{3,2,1,0:T(8,128)} fusion(f32[8,8,64,256]{3,2,1,0:T(8,128)} %param.33, s32[1024]{0:T(1024)S(1)} %pad_clamp_fusion), kind=kCustom, calls=%fused_computation.2 | custom fusion | bytes 16777280 | tf_op jit(solution)/shard_map/gather | solution.py:133
  26.0 6.6 %all-to-all-start.1 = ((f32[16,3,512]{2,1,0:T(4,128)}), f32[16,3,512]{2,1,0:T(4,128)S(1)}, u32[]{:S(2)}, u32[]{:S(2)}) async-start(f32[16,3,512]{2,1,0:T(4,128)} %copy.44), calls=%async_computation.1 | async-start | bytes 262144 | tf_op jit(solution)/shard_map/all_to_all | solution.py:138
  32.7 8.4 %broadcast_select_fusion = f32[16,8,64,256]{3,2,1,0:T(8,128)} fusion(f32[16,8,64,256]{3,2,1,0:T(8,128)} %gather_fusion.2, pred[16]{0:T(512)(128)(4,1)S(1)} %fusion.71), kind=kLoop, calls=%fused_computation.5 | loop fusion | flops 2097152 | bytes 16777232 | tf_op jit(solution)/shard_map/jit(_where)/select_n | solution.py:133
  41.1 6.6 %all-to-all-start.3 = ((f32[16,8,64,256]{3,2,1,0:T(8,128)}), f32[16,8,64,256]{3,2,1,0:T(8,128)}, u32[]{:S(2)}, u32[]{:S(2)}) async-start(f32[16,8,64,256]{3,2,1,0:T(8,128)} %broadcast_select_fusion), calls=%async_computation.3 | async-start | bytes 16777216 | tf_op jit(solution)/shard_map/all_to_all | solution.py:137
  47.7 1.9 copy.42
  49.7 92.0 %all-to-all-done.3 = f32[16,8,64,256]{3,2,1,0:T(8,128)} async-done(((f32[16,8,64,256]{3,2,1,0:T(8,128)}), f32[16,8,64,256]{3,2,1,0:T(8,128)}, u32[]{:S(2)}, u32[]{:S(2)}) %all-to-all-start.3) | async-done | bytes 8388640 | tf_op jit(solution)/shard_map/all_to_all | solution.py:137
  141.7 5.9 %stack.2 = bf16[8,1024,2,512]{3,1,2,0:T(8,128)(2,1)} broadcast(bf16[1024,2,512]{2,0,1:T(8,128)(2,1)S(1)} %copy.42), dimensions={1,2,3} | broadcast | bytes 18874368 | tf_op jit(solution)/shard_map/stack | solution.py:13
  147.6 5.9 %all-to-all-start = ((bf16[8,1024,2,512]{3,1,2,0:T(8,128)(2,1)}), bf16[8,1024,2,512]{3,1,2,0:T(8,128)(2,1)}, u32[]{:S(2)}, u32[]{:S(2)}) async-start(bf16[8,1024,2,512]{3,1,2,0:T(8,128)(2,1)} %stack.2), calls=%async_computation | async-start | bytes 33554432 | tf_op jit(solution)/shard_map/all_to_all | solution.py:14
  155.1 217.0 %all_gather.10 = bf16[8192,8]{0,1:T(8,128)(2,1)S(1)} all-gather(bf16[1024,8]{0,1:T(8,128)(2,1)S(1)} %copy-done.4), channel_id=1, replica_groups=mesh['wide'=32,'req'=8] {'req'}, dimensions={0}, use_global_device_ids=true | all-gather | bytes 147456 | tf_op jit(solution)/shard_map/all_gather | solution.py:117
  374.6 4.3 reduce_sum.64
  379.0 51.7 %all-gather.3.cloned.1.call-done = bf16[256,8192]{1,0:T(8,128)(2,1)} async-done(((bf16[256,256]{1,0:T(8,128)(2,1)}), bf16[256,8192]{1,0:T(8,128)(2,1)}) %all-gather.3.cloned.1.call-update) | async-done | bytes 4194320 | tf_op jit(solution)/shard_map/all_gather | solution.py:108
  430.8 4.5 fusion.7
  435.9 1.2 compare_select_fusion
  437.7 1.2 collective-permute-start.1
  439.1 3.7 collective-permute-done.1
  443.6 0.9 fusion.12
  444.6 0.9 fusion.44
  445.5 8.2 %copy.43 = bf16[8,1024,2,512]{3,1,0,2:T(8,128)(2,1)S(1)} copy(bf16[8,1024,2,512]{3,1,2,0:T(8,128)(2,1)} %all-to-all-done) | data formatting | bytes 33554432 | tf_op jit(solution)/shard_map/all_to_all | solution.py:14
  453.8 4.5 fusion.2
  458.3 0.9 slice_convert_fusion
  460.0 0.8 slice_bitcast_fusion.1
  460.9 0.9 slice_bitcast_fusion.5
  461.7 2.0 copy.53
  463.8 3.0 multiply_convert_fusion.4
  466.7 1.1 copy.47
  467.8 2.2 multiply_reduce_fusion
  470.1 1.2 collective-permute-start.2
  472.1 0.9 collective-permute-start.3
  473.0 1.3 convolution_add_fusion
  474.6 0.9 fusion.34
  (79 shorter events, 11.6 us)
Async XLA Ops:
  7.2 10.8 %copy-start = (bf16[8,3,512]{2,0,1:T(8,128)(2,1)S(1)}, bf16[8,3,512]{2,0,1:T(8,128)(2,1)}, u32[]{:S(2)}) copy-start(bf16[8,3,512]{2,0,1:T(8,128)(2,1)} %param.34) | copy-start | bytes 73732
  10.5 15.5 %all-to-all-start.2 = ((f32[16,3,128]{2,1,0:T(4,128)}), f32[16,3,128]{2,1,0:T(4,128)S(1)}, u32[]{:S(2)}, u32[]{:S(2)}) async-start(f32[16,3,128]{2,1,0:T(4,128)} %copy.48), calls=%async_computation.2 | async-start | bytes 65536 | tf_op jit(solution)/shard_map/all_to_all | solution.py:139
  26.0 15.0 %all-to-all-start.1 = ((f32[16,3,512]{2,1,0:T(4,128)}), f32[16,3,512]{2,1,0:T(4,128)S(1)}, u32[]{:S(2)}, u32[]{:S(2)}) async-start(f32[16,3,512]{2,1,0:T(4,128)} %copy.44), calls=%async_computation.1 | async-start | bytes 262144 | tf_op jit(solution)/shard_map/all_to_all | solution.py:138
  41.1 100.6 %all-to-all-start.3 = ((f32[16,8,64,256]{3,2,1,0:T(8,128)}), f32[16,8,64,256]{3,2,1,0:T(8,128)}, u32[]{:S(2)}, u32[]{:S(2)}) async-start(f32[16,8,64,256]{3,2,1,0:T(8,128)} %broadcast_select_fusion), calls=%async_computation.3 | async-start | bytes 16777216 | tf_op jit(solution)/shard_map/all_to_all | solution.py:137
  147.6 7.5 %copy-start.4 = (bf16[1024,8]{0,1:T(8,128)(2,1)S(1)}, bf16[1024,8]{0,1:T(8,128)(2,1)}, u32[]{:S(2)}) copy-start(bf16[1024,8]{0,1:T(8,128)(2,1)} %param.20) | copy-start | bytes 49156
  147.6 224.5 %copy-start.11 = (s32[1,2]{1,0:T(1,128)S(1)}, s32[1,2]{1,0:T(1,128)}, u32[]{:S(2)}) copy-start(s32[1,2]{1,0:T(1,128)} %param.30) | copy-start | bytes 28
  147.6 224.6 %copy-start.12 = (s32[2]{0:T(128)S(1)}, s32[2]{0:T(128)}, u32[]{:S(2)}) copy-start(s32[2]{0:T(128)} %param.31) | copy-start | bytes 28
  147.6 224.7 %copy-start.13 = (f32[8]{0:T(128)S(1)}, f32[8]{0:T(128)}, u32[]{:S(2)}) copy-start(f32[8]{0:T(128)} %param.23) | copy-start | bytes 100
  147.6 224.7 %copy-start.9 = (f32[4,128]{1,0:T(4,128)S(1)}, f32[4,128]{1,0:T(4,128)}, u32[]{:S(2)}) copy-start(f32[4,128]{1,0:T(4,128)} %param.27) | copy-start | bytes 6148
  147.6 224.7 %copy-start.5 = (f32[4,512]{1,0:T(4,128)S(1)}, f32[4,512]{1,0:T(4,128)}, u32[]{:S(2)}) copy-start(f32[4,512]{1,0:T(4,128)} %param.25) | copy-start | bytes 24580
  147.6 297.9 %all-to-all-start = ((bf16[8,1024,2,512]{3,1,2,0:T(8,128)(2,1)}), bf16[8,1024,2,512]{3,1,2,0:T(8,128)(2,1)}, u32[]{:S(2)}, u32[]{:S(2)}) async-start(bf16[8,1024,2,512]{3,1,2,0:T(8,128)(2,1)} %stack.2), calls=%async_computation | async-start | bytes 33554432 | tf_op jit(solution)/shard_map/all_to_all | solution.py:14
  153.5 225.5 %all-gather.5.cloned.1.call-start = ((), (), s32[]{:S(2)}) async-start(), calls=%async_computation.5 | async-start | bytes 2359296 | tf_op jit(solution)/shard_map/all_gather | solution.py:122
  154.3 276.5 %all-gather.3.cloned.1.call-start = ((), (), s32[]{:S(2)}) async-start(), calls=%async_computation.4 | async-start | bytes 4325376 | tf_op jit(solution)/shard_map/all_gather | solution.py:108
  379.0 56.3 %copy-start.10 = (f32[128]{0:T(128)S(1)}, f32[128]{0:T(128)}, u32[]{:S(2)}) copy-start(f32[128]{0:T(128)} %param.28) | copy-start | bytes 1540
  379.0 57.0 %copy-start.8 = (f32[8]{0:T(128)S(1)}, f32[8]{0:T(128)}, u32[]{:S(2)}) copy-start(f32[8]{0:T(128)} %param.22) | copy-start | bytes 100
  430.8 5.2 %copy-start.2 = (bf16[256,8192]{1,0:T(8,128)(2,1)S(1)}, bf16[256,8192]{1,0:T(8,128)(2,1)}, u32[]{:S(2)}) copy-start(bf16[256,8192]{1,0:T(8,128)(2,1)} %all-gather.3.cloned.1.call-done) | copy-start | bytes 12582916
  435.6 2.1 collective-permute-start
  437.7 5.1 %collective-permute-start.1 = (bf16[256,256]{0,1:T(8,128)(2,1)S(1)}, bf16[256,256]{0,1:T(8,128)(2,1)S(1)}, u32[]{:S(2)}, u32[]{:S(2)}) collective-permute-start(bf16[256,256]{0,1:T(8,128)(2,1)S(1)} %maximum_select_fusion.1), channel_id=1, source_target_pairs={{0,16},{16,0},{8,24},{24,8},{32,48},{48,32},{40,56},{56,40},{64,80... | collective-permute-start | bytes 393224 | tf_op jit(solution)/shard_map/ppermute | solution.py:24
  445.5 8.3 %copy-start.3 = (bf16[256,8192]{1,0:T(8,128)(2,1)S(1)}, bf16[256,8192]{1,0:T(8,128)(2,1)}, u32[]{:S(2)}) copy-start(bf16[256,8192]{1,0:T(8,128)(2,1)} %all-gather.3.cloned.1.call-done) | copy-start | bytes 12582916
  458.3 5.5 %copy-start.6 = (f32[512]{0:T(512)S(1)}, f32[512]{0:T(512)}, u32[]{:S(2)}) copy-start(f32[512]{0:T(512)} %param.26) | copy-start | bytes 6148
  459.2 8.6 %copy-start.14 = (f32[8]{0:T(128)S(1)}, f32[8]{0:T(128)}, u32[]{:S(2)}) copy-start(f32[8]{0:T(128)} %param.24) | copy-start | bytes 100
  467.8 6.7 %copy-start.7 = (f32[512]{0:T(512)S(1)}, f32[512]{0:T(512)}, u32[]{:S(2)}) copy-start(f32[512]{0:T(512)} %param.29) | copy-start | bytes 6148
  467.8 7.6 %copy-start.1 = (bf16[8,3,512]{2,0,1:T(8,128)(2,1)S(1)}, bf16[8,3,512]{2,0,1:T(8,128)(2,1)}, u32[]{:S(2)}) copy-start(bf16[8,3,512]{2,0,1:T(8,128)(2,1)} %param.34) | copy-start | bytes 73732
  470.1 2.0 collective-permute-start.2
  472.1 2.5 collective-permute-start.3
Sparse Core Ops, SparseCore 0:
  157.0 200.3 all-gather.4
  359.1 71.5 all-gather.2
